TPU v7x, 32 devices: a whole 2x2x4 slice. The times are simulated.
32 devices in a mesh: chan: 16 (over z, x, core), tm: 2 (over y).
Axes of the slice: x: 2, y: 2, z: 4, core: 2. Of those that a mesh axis runs over, the one named last changes fastest.
Arguments:
- traces: bfloat16 [512, 4, 2048], P('chan', None, 'tm'), may hold values from -40 to 40
- delays: int32 [128, 512], P(None, 'chan'), may hold values from 0 to 1023
- offsets: int32 [4], P('tm'), may hold values from 0 to 2047
Outputs:
- brightness: float32 [4, 128, 256], P('tm', 'chan')
All inputs are finite; a program needn't handle non-finite values.
Results may differ from a plain program's by a relative error of at most 0.0048.
Values may be sent and summed in bfloat16 or wider, within the bound.
A program may use at most 64 MiB of HBM per device.

v0:
```python
import functools
import math

import jax
import jax.numpy as jnp
from jax import lax
from jax.experimental import pallas as pl
from jax.experimental.pallas import tpu as pltpu
from jax.sharding import PartitionSpec as P

SAMPLES = 2048
BAND = 512
FB = 128
TB = 256
BAND_LO = 128
DEC = 8
STEP = 32
PAIR = 2

epsilon = 1e-06
full_turn = 2.0 * math.pi
MESH = pl.DeviceIdType.MESH


COS_TURN = (
    0.9999999890590201, -19.739204499453688, 64.93911745988827, -85.45013953077586,
    60.16763095018129, -25.96759924584206, 6.528658157862129,
)
SIN_TURN = (
    6.283185302511498, -41.341700405316736, 81.60513138576982, -76.70301535347629,
    42.02592698341473, -14.899846660399582, 3.2381375010236435,
)


def cos_sin(turns):
    x = turns - jnp.round(turns)
    y = x * x
    c, s = COS_TURN[-1], SIN_TURN[-1]
    for c_next, s_next in zip(COS_TURN[-2::-1], SIN_TURN[-2::-1]):
        c = c * y + c_next
        s = s * y + s_next
    return c, s * x


def float_iota(shape, axis):
    return lax.broadcasted_iota(jnp.int32, shape, axis).astype(jnp.float32)


def bit_of(value, at):
    return lax.rem(value // (1 << at), 2)


def flip(value, at):
    return value + (1 - 2 * bit_of(value, at)) * (1 << at)


def parity_row(first, width):
    ids = first + lax.broadcasted_iota(jnp.int32, (1, width), 1)
    return (1 - 2 * (ids & 1)).astype(jnp.float32)


def kernel(
    n_chan, x_ref, d_hbm, off_hbm, out_ref,
    d_ref, other, base_c, base_s, lead_c, lead_s, fwd, inv, env, phase_c, phase_s,
    nodes_d, turn_tab, turn_row, e_tab, send_buf, recv_buf,
    off_ref, off_sem, d_sem, x_send, x_recv, send_sem, recv_sem, round_sem,
):
    windows, chans, half = x_ref.shape
    kept = windows // 2
    rows = kept * chans
    nodes = d_hbm.shape[1]
    node_rows = nodes // n_chan
    me = lax.axis_index("chan")
    tm = lax.axis_index("tm")
    partner = 1 - tm

    offsets_in = pltpu.make_async_copy(off_hbm, off_ref, off_sem)
    delays_in = pltpu.make_async_copy(d_hbm, d_ref, d_sem)
    delays_in.start()
    offsets_in.start()

    rounds = n_chan.bit_length() - 1
    barrier = pltpu.get_barrier_semaphore()
    pl.semaphore_signal(barrier, inc=1, device_id={"tm": partner}, device_id_type=MESH)
    for r in range(rounds):
        pl.semaphore_signal(barrier, inc=1, device_id={"chan": flip(me, r)}, device_id_type=MESH)

    def tell(r):
        if r < rounds:
            pl.semaphore_signal(round_sem.at[r], inc=1, device_id={"chan": flip(me, r)}, device_id_type=MESH)

    def hear(r):
        if r < rounds:
            pl.semaphore_wait(round_sem.at[r], 1)
            tell(r + 1)

    width = BAND + FB
    tiles = BAND // 128
    side_tiles = tiles // 2
    side_band = BAND // 2
    leads = half // STEP
    unit = 1.0 / SAMPLES
    for q in range(width // 128):
        cols = slice(q * 128, (q + 1) * 128)
        if q < tiles:
            freq = (2.0 * float_iota((1, 128), 1) + (BAND_LO + q % side_tiles * 256 + q // side_tiles)) * unit
        else:
            freq = (float_iota((1, 128), 1) + (1 + (q - tiles) * 128)) * unit
        base_c[:, cols], base_s[:, cols] = cos_sin(float_iota((STEP, 128), 0) * freq)
        lead_c[q], lead_s[q] = cos_sin(float_iota((leads, 128), 0) * (freq * STEP))

    place = float_iota((1, side_band), 1) * 2.0
    place = jnp.concatenate([place, place + 1.0], axis=1)
    taper_angle = math.pi * (place + 0.5) / BAND
    weight = 2.0 * jnp.sin(taper_angle) ** 2 / SAMPLES

    pl.semaphore_wait(barrier, rounds + 1)
    exchange = pltpu.make_async_remote_copy(
        src_ref=x_ref.at[pl.ds(partner * kept, kept)],
        dst_ref=other,
        send_sem=x_send,
        recv_sem=x_recv,
        device_id={"tm": partner},
        device_id_type=MESH,
    )
    exchange.start()

    tell(0)

    @pl.loop(0, half // STEP)
    def _(a):
        at = pl.ds(pl.multiple_of(a * STEP, STEP), STEP)
        for q in range(width // 128):
            cols = slice(q * 128, (q + 1) * 128)
            ca, sa = lead_c[q, pl.ds(a, 1), :], lead_s[q, pl.ds(a, 1), :]
            cb, sb = base_c[:, cols], base_s[:, cols]
            c = ca * cb - sa * sb
            s = sa * cb + ca * sb
            if q * 128 < BAND:
                g = weight[:, cols]
                high = slice(BAND + q * 128, BAND + (q + 1) * 128)
                fwd[at, cols] = c.astype(jnp.bfloat16)
                fwd[at, high] = (-s).astype(jnp.bfloat16)
                to = q // side_tiles * BAND + q % side_tiles * 128
                inv[at, to : to + 128] = (g * c).astype(jnp.bfloat16)
                inv[at, to + side_band : to + side_band + 128] = (g * s).astype(jnp.bfloat16)
            else:
                low = slice(q * 128 - BAND, (q + 1) * 128 - BAND)
                high = slice(FB + low.start, FB + low.stop)
                env[at, low] = c.astype(jnp.bfloat16)
                env[at, high] = (-s).astype(jnp.bfloat16)

    hear(0)

    delays_in.wait()
    nodes_d[...] = (d_ref[...].astype(jnp.float32) * unit).T
    block = PAIR * node_rows
    env_bins = 1.0 + float_iota((1, FB), 1)

    pairs = n_chan // PAIR
    ahead = (pairs + 1) // 2
    my_pair = me // PAIR

    def pair_at(step):
        mask = pairs - 1 - step
        found = 0
        for at in range(rounds - 1):
            found = found + lax.rem(bit_of(my_pair, at) + bit_of(mask, at), 2) * (1 << at)
        return found

    def phases(step):
        at = pl.ds(pl.multiple_of(pair_at(step) * block, block), block)
        delay = nodes_d[at, :]
        for ch in range(chans):
            c, s = cos_sin(delay[:, ch : ch + 1] * env_bins)
            phase_c[ch, at, :] = c.astype(jnp.bfloat16)
            phase_s[ch, at, :] = s.astype(jnp.bfloat16)

    pl.loop(0, ahead)(phases)
    hear(1)
    hear(2)

    own = x_ref[pl.ds(tm * kept, kept)].reshape(rows, half)
    own_terms = jnp.dot(own, fwd[...], preferred_element_type=jnp.float32)
    exchange.wait()
    other_terms = jnp.dot(other[...].reshape(rows, half), fwd[...], preferred_element_type=jnp.float32)
    late_sign = jnp.where((lax.broadcasted_iota(jnp.int32, (1, side_band), 1) * 0 + tm) == 1, -1.0, 1.0)

    def spectrum(first, odd):
        cols = slice(first, first + side_band)
        mine, theirs = own_terms[:, cols], other_terms[:, cols]
        both = (mine - theirs) * late_sign if odd else mine + theirs
        return both.astype(jnp.bfloat16).astype(jnp.float32)

    def analytic(odd):
        re, im = spectrum(odd * side_band, odd), spectrum(BAND + odd * side_band, odd)
        left = jnp.concatenate([re, im], axis=0)
        right = jnp.concatenate([-im, re], axis=0)
        return lax.dot_general(
            jnp.concatenate([left, right], axis=1).astype(jnp.bfloat16),
            inv[:, odd * BAND : (odd + 1) * BAND],
            (((1,), (1,)), ((), ())),
            preferred_element_type=jnp.float32,
        )

    even_part, odd_part = analytic(0), analytic(1)
    early, late = even_part + odd_part, even_part - odd_part
    real_part = jnp.concatenate([early[:rows], late[:rows]], axis=0)
    imag_part = jnp.concatenate([early[rows:], late[rows:]], axis=0)
    energy = real_part * real_part + imag_part * imag_part
    sums = jnp.sum(energy, axis=1, keepdims=True)
    sums = sums[:rows] + sums[rows:]
    spread = jnp.dot(energy.astype(jnp.bfloat16), env[...], preferred_element_type=jnp.float32)
    spread = spread[:rows] + spread[rows:] * parity_row(1, 2 * FB)
    factor = 1.0 / (math.sqrt(SAMPLES) * (sums / SAMPLES + epsilon))
    e_tab[...] = (spread * factor).astype(jnp.bfloat16).astype(jnp.float32)

    for r in range(3, rounds):
        hear(r)

    def outgoing(dest):
        return pltpu.make_async_remote_copy(
            src_ref=send_buf.at[dest],
            dst_ref=recv_buf.at[me],
            send_sem=send_sem.at[dest],
            recv_sem=recv_sem.at[me],
            device_id={"chan": dest},
            device_id_type=MESH,
        )

    def send_pair(step):
        for side in range(PAIR):
            dest = pair_at(step) * PAIR + side

            @pl.when(dest != me)
            def _():
                outgoing(dest).start()

    @pl.loop(0, pairs)
    def _(step):
        @pl.when(step >= ahead)
        def _():
            phases(step)

        pair = pair_at(step)
        at = pl.ds(pl.multiple_of(pair * block, block), block)
        acc = [[jnp.zeros((block, FB), jnp.float32) for _ in range(kept)] for _ in range(2)]
        for ch in range(chans):
            pc = phase_c[ch, at, :].astype(jnp.float32)
            ps = phase_s[ch, at, :].astype(jnp.float32)
            for w in range(kept):
                r = w * chans + ch
                er, ei = e_tab[r : r + 1, :FB], e_tab[r : r + 1, FB:]
                acc[0][w] = acc[0][w] + (pc * er - ps * ei)
                acc[1][w] = acc[1][w] + (pc * ei + ps * er)
        for side in range(PAIR):
            part = slice(side * node_rows, (side + 1) * node_rows)
            packed = jnp.concatenate([acc[p][w][part] for p in range(2) for w in range(kept)], axis=0)
            send_buf[pair * PAIR + side] = packed.astype(jnp.bfloat16)

        @pl.when(step > 0)
        def _():
            send_pair(step - 1)

    send_pair(pairs - 1)

    c, s = cos_sin((1.0 + float_iota((FB, TB), 0)) * (float_iota((FB, TB), 1) * (DEC * unit)))
    turn_tab[:FB, :] = c
    turn_tab[FB:, :] = -s
    offsets_in.wait()
    for w in range(kept):
        shift = off_ref[w].astype(jnp.float32) * unit
        turn_row[w, :, :FB], turn_row[w, :, FB:] = cos_sin(env_bins * shift)

    def incoming(source):
        return pltpu.make_async_remote_copy(
            src_ref=send_buf.at[source],
            dst_ref=recv_buf.at[source],
            send_sem=send_sem.at[source],
            recv_sem=recv_sem.at[source],
            device_id={"chan": source},
            device_id_type=MESH,
        )

    def add_one(source, stack):
        incoming(source).wait_recv()
        return stack + recv_buf[source].astype(jnp.float32)

    def add_pair(step, stack):
        for side in range(PAIR):
            stack = add_one(pair_at(step) * PAIR + side, stack)
        return stack

    stack = lax.fori_loop(0, pairs - 1, add_pair, send_buf[me].astype(jnp.float32))
    stack = add_one(flip(me, 0), stack)

    turned = []
    for w in range(kept):
        c, s = turn_row[w, :, :FB], turn_row[w, :, FB:]
        re = stack[w * node_rows : (w + 1) * node_rows]
        im = stack[(kept + w) * node_rows : (kept + w + 1) * node_rows]
        turned.append(jnp.concatenate([re * c - im * s, re * s + im * c], axis=1))
    bright = jnp.dot(
        jnp.concatenate(turned, axis=0), turn_tab[...],
        precision=lax.Precision.HIGHEST, preferred_element_type=jnp.float32,
    )
    scale = 1.0 / math.sqrt(FB * chans * n_chan)
    out_ref[...] = (bright * scale).reshape(kept, node_rows, TB)

    @pl.loop(1, n_chan)
    def _(step):
        outgoing(lax.rem(me + step, n_chan)).wait_send()


def solution(mesh):
    n_chan = mesh.shape["chan"]

    def on_device(traces, delays, offsets):
        chans, windows, half = traces.shape
        nodes = delays.shape[0]
        kept = offsets.shape[0]
        node_rows = nodes // n_chan
        by_window = jnp.transpose(traces, (1, 0, 2))
        vmem = pl.BlockSpec(memory_space=pltpu.VMEM)
        packed_rows = 2 * kept * node_rows
        return pl.pallas_call(
            functools.partial(kernel, n_chan),
            out_shape=jax.ShapeDtypeStruct((kept, node_rows, TB), jnp.float32),
            in_specs=[vmem] + [pl.BlockSpec(memory_space=pltpu.HBM)] * 2,
            out_specs=vmem,
            scratch_shapes=[
                pltpu.VMEM((chans, nodes), jnp.int32),
                pltpu.VMEM((kept, chans, half), jnp.bfloat16),
                pltpu.VMEM((STEP, BAND + FB), jnp.float32),
                pltpu.VMEM((STEP, BAND + FB), jnp.float32),
                pltpu.VMEM(((BAND + FB) // 128, half // STEP, 128), jnp.float32),
                pltpu.VMEM(((BAND + FB) // 128, half // STEP, 128), jnp.float32),
                pltpu.VMEM((half, 2 * BAND), jnp.bfloat16),
                pltpu.VMEM((half, 2 * BAND), jnp.bfloat16),
                pltpu.VMEM((half, 2 * FB), jnp.bfloat16),
                pltpu.VMEM((chans, nodes, FB), jnp.bfloat16),
                pltpu.VMEM((chans, nodes, FB), jnp.bfloat16),
                pltpu.VMEM((nodes, chans), jnp.float32),
                pltpu.VMEM((2 * FB, TB), jnp.float32),
                pltpu.VMEM((kept, 1, 2 * FB), jnp.float32),
                pltpu.VMEM((kept * chans, 2 * FB), jnp.float32),
                pltpu.VMEM((n_chan, packed_rows, FB), jnp.bfloat16),
                pltpu.VMEM((n_chan, packed_rows, FB), jnp.bfloat16),
                pltpu.SMEM((kept,), jnp.int32),
                pltpu.SemaphoreType.DMA,
                pltpu.SemaphoreType.DMA,
                pltpu.SemaphoreType.DMA,
                pltpu.SemaphoreType.DMA,
                pltpu.SemaphoreType.DMA((n_chan,)),
                pltpu.SemaphoreType.DMA((n_chan,)),
                pltpu.SemaphoreType.REGULAR((n_chan.bit_length() - 1,)),
            ],
            compiler_params=pltpu.CompilerParams(
                collective_id=0, has_side_effects=True, vmem_limit_bytes=16 * 1024 * 1024 + 4 * chans * nodes * FB
            ),
        )(by_window, *(pltpu.with_memory_space_constraint(a, pltpu.HBM) for a in (delays.T, offsets)))

    placed = (P("chan", None, "tm"), P(None, "chan"), P("tm"))
    return jax.shard_map(
        on_device, mesh=mesh, in_specs=placed, out_specs=P("tm", "chan", None), check_vma=False
    )
```

profile of v0, /device:TPU:0, one launch (start us, length us, event | category | flops | bytes accessed | tf_op | source)
XLA Modules:
  0.0 19.0 jit_solution(8077747722375651937)
XLA Ops:
  0.0 1.0 %copy.6 = bf16[32,4,1024]{2,0,1:T(8,128)(2,1)S(1)} copy(bf16[32,4,1024]{2,1,0:T(4,128)(2,1)} %param.3) | data formatting | bytes 524288 | tf_op args[0]
  1.0 17.4 %shard_map.37 = f32[2,8,256]{2,1,0:T(8,128)S(1)} custom-call(bf16[4,32,1024]{2,1,0:T(8,128)(2,1)S(1)} %bitcast.4, s32[32,128]{1,0:T(8,128)} %bitcast.5, s32[2]{0:T(128)} %off_hbm.1), custom_call_target="tpu_custom_call" | custom-call | tf_op jit(solution)/shard_map/pallas_call | solution.py:326
  18.4 0.6 %copy.8 = f32[2,8,256]{2,1,0:T(8,128)} copy(f32[2,8,256]{2,1,0:T(8,128)S(1)} %shard_map.37) | data formatting | bytes 32768
where the time goes:
time: 19.1 us; the launch traced here: 19 us
  Pallas kernels  17.4 us (91%)
  local copies, waits for them, and re-layouts  1.64 us (9%)
    pallas_call x1, Pallas kernels, on_device(): pl.pallas_call(functools.partial(kernel, n_chan), out_shape=jax.ShapeDtyp...  17.4 us
    unnamed x2, local copies, waits for them, and re-layouts  1.64 us

commit v1 on v0

v1 whole, which is shorter than its diff:
```python
import functools
import math

import jax
import jax.numpy as jnp
from jax import lax
from jax.experimental import pallas as pl
from jax.experimental.pallas import tpu as pltpu
from jax.sharding import PartitionSpec as P

SAMPLES = 2048
BAND = 512
FB = 128
TB = 256
BAND_LO = 128
DEC = 8
PAIR = 2
CHUNKS = 4

RADIX = 8
SPAN = SAMPLES // RADIX
BINS = BAND // RADIX
TIMES = SAMPLES // 2
FOLD = TIMES // 2
INNER = TIMES // RADIX
HALF_FB = FB // 2

epsilon = 1e-06
full_turn = 2.0 * math.pi
root_half = math.sqrt(0.5)
MESH = pl.DeviceIdType.MESH


COS_TURN = (
    0.9999999890590201, -19.739204499453688, 64.93911745988827, -85.45013953077586,
    60.16763095018129, -25.96759924584206, 6.528658157862129,
)
SIN_TURN = (
    6.283185302511498, -41.341700405316736, 81.60513138576982, -76.70301535347629,
    42.02592698341473, -14.899846660399582, 3.2381375010236435,
)


def cos_sin(turns):
    x = turns - jnp.round(turns)
    y = x * x
    c, s = COS_TURN[-1], SIN_TURN[-1]
    for c_next, s_next in zip(COS_TURN[-2::-1], SIN_TURN[-2::-1]):
        c = c * y + c_next
        s = s * y + s_next
    return c, s * x


def float_iota(shape, axis):
    return lax.broadcasted_iota(jnp.int32, shape, axis).astype(jnp.float32)


def bit_of(value, at):
    return lax.rem(value // (1 << at), 2)


def flip(value, at):
    return value + (1 - 2 * bit_of(value, at)) * (1 << at)


def split(value):
    high = value.astype(jnp.bfloat16)
    return high, (value - high.astype(jnp.float32)).astype(jnp.bfloat16)


def env_bins(axis):
    shape = (1, FB) if axis else (FB, 1)
    lane = lax.broadcasted_iota(jnp.int32, shape, axis)
    return jnp.where(lane < HALF_FB, 2 * lane + 2, 2 * lane - (FB - 1)).astype(jnp.float32)


def inverse_four(values):
    (ar, ai), (br, bi), (cr, ci), (dr, di) = values
    sr, si, er, ei = ar + cr, ai + ci, ar - cr, ai - ci
    tr, ti, fr, fi = br + dr, bi + di, br - dr, bi - di
    return [(sr + tr, si + ti), (er - fi, ei + fr), (sr - tr, si - ti), (er + fi, ei - fr)]


def kernel(
    n_chan, x_hbm, d_hbm, off_hbm, out_ref,
    d_ref, own, other, fwd, inv, env, fwd_c, fwd_s, inv_c, inv_s, gain, phase_c, phase_s,
    nodes_d, turn_tab, turn_row, e_tab, acc, send_buf, recv_buf,
    off_ref, off_sem, d_sem, x_in, x_send, x_recv, send_sem, recv_sem, round_sem,
):
    chans, kept, half = own.shape
    group = chans // CHUNKS
    rows = kept * group
    nodes = d_hbm.shape[1]
    node_rows = nodes // n_chan
    me = lax.axis_index("chan")
    tm = lax.axis_index("tm")
    partner = 1 - tm
    unit = 1.0 / SAMPLES

    rounds = n_chan.bit_length() - 1
    barrier = pltpu.get_barrier_semaphore()
    pl.semaphore_signal(barrier, inc=1, device_id={"tm": partner}, device_id_type=MESH)
    for r in range(rounds):
        pl.semaphore_signal(barrier, inc=1, device_id={"chan": flip(me, r)}, device_id_type=MESH)

    offsets_in = pltpu.make_async_copy(off_hbm, off_ref, off_sem)
    delays_in = pltpu.make_async_copy(d_hbm, d_ref, d_sem)
    own_in = pltpu.make_async_copy(
        x_hbm.at[:, pl.ds(pl.multiple_of(tm * kept, kept), kept)], own, x_in
    )
    delays_in.start()
    offsets_in.start()
    own_in.start()

    def tell(r):
        if r < rounds:
            pl.semaphore_signal(round_sem.at[r], inc=1, device_id={"chan": flip(me, r)}, device_id_type=MESH)

    def hear(r):
        if r < rounds:
            pl.semaphore_wait(round_sem.at[r], 1)
            tell(r + 1)

    def exchange(first, count, at):
        return pltpu.make_async_remote_copy(
            src_ref=x_hbm.at[pl.ds(first, count), pl.ds(pl.multiple_of(partner * kept, kept), kept)],
            dst_ref=other.at[pl.ds(first, count)],
            send_sem=x_send,
            recv_sem=x_recv.at[at],
            device_id={"tm": partner},
            device_id_type=MESH,
        )

    pl.semaphore_wait(barrier, rounds + 1)
    for g in range(CHUNKS):
        exchange(g * group, group, g).start()
    tell(0)

    late = jnp.where(lax.broadcasted_iota(jnp.int32, (1, SPAN), 1) * 0 + tm == 1, -1.0, 1.0)
    residue = lax.broadcasted_iota(jnp.int32, (RADIX, SPAN), 0)
    c, s = cos_sin(residue.astype(jnp.float32) * float_iota((RADIX, SPAN), 1) * unit)
    sign = jnp.where((residue & 1) == 1, late, 1.0)
    fwd_c[...] = c * sign
    fwd_s[...] = s * sign
    inv_c[...], inv_s[...] = cos_sin(float_iota((RADIX, INNER), 0) * float_iota((RADIX, INNER), 1) * (1.0 / TIMES))
    lane = lax.broadcasted_iota(jnp.int32, (1, 2 * BINS), 1)
    quarter = jnp.where(lane < BINS, 0.0, 0.25)
    place = jnp.where(lane < BINS, lane, lane - BINS).astype(jnp.float32)
    _, s = cos_sin((RADIX * place + float_iota((RADIX, 2 * BINS), 0) + 0.5) * (0.5 / BAND))
    gain[...] = s * s * (2.0 / SAMPLES)

    def forward_table(at):
        first = pl.multiple_of(at * 32, 32)
        spot = float_iota((32, 2 * BINS), 0) + first.astype(jnp.float32)
        c, s = cos_sin(spot * ((place + BAND_LO // RADIX) * (1.0 / SPAN)) + quarter)
        for value, base in ((c, 0), (s, SPAN)):
            high, low = split(value)
            fwd[pl.ds(pl.multiple_of(base + first, 32), 32), : 2 * BINS] = high
            fwd[pl.ds(pl.multiple_of(base + first, 32), 32), 2 * BINS :] = low

    pl.loop(0, SPAN // 32)(forward_table)

    row = lax.broadcasted_iota(jnp.int32, (2 * BINS, 1), 0)
    row_quarter = jnp.where(row < BINS, 0.0, 0.25)
    row_place = jnp.where(row < BINS, row, row - BINS).astype(jnp.float32)
    c, s = cos_sin(row_place * (float_iota((1, INNER), 1) * (1.0 / INNER)) + row_quarter)
    for base in (0, 2 * BINS):
        inv[base : base + 2 * BINS, :INNER] = c.astype(jnp.bfloat16)
        inv[base : base + 2 * BINS, INNER:] = s.astype(jnp.bfloat16)

    env_lane = lax.broadcasted_iota(jnp.int32, (1, FB), 1)
    env_quarter = jnp.where(env_lane < HALF_FB, 0.0, 0.25)
    env_place = jnp.where(env_lane < HALF_FB, env_lane, env_lane - HALF_FB).astype(jnp.float32)
    for odd in range(2):
        freq = (2.0 * env_place + (1.0 if odd else 2.0)) * (1.0 / TIMES)
        base_c, base_s = cos_sin(float_iota((32, FB), 0) * freq + env_quarter)
        lead_c, lead_s = cos_sin(float_iota((FOLD // 32, FB), 0) * (freq * 32.0))
        for a in range(FOLD // 32):
            value = lead_c[a : a + 1] * base_c - lead_s[a : a + 1] * base_s
            env[odd, a * 32 : (a + 1) * 32, :] = value.astype(jnp.bfloat16)

    hear(0)

    delays_in.wait()
    nodes_d[...] = (d_ref[...].astype(jnp.float32) * unit).T
    block = PAIR * node_rows
    bins = env_bins(1)
    pairs = n_chan // PAIR

    def phases(step):
        at = pl.ds(pl.multiple_of(step * block, block), block)
        delay = nodes_d[at, :]
        for ch in range(chans):
            c, s = cos_sin(delay[:, ch : ch + 1] * bins)
            phase_c[ch, at, :] = c
            phase_s[ch, at, :] = s
        acc[step] = jnp.zeros(acc.shape[1:], jnp.float32)

    pl.loop(0, pairs // 2)(phases)
    hear(1)
    pl.loop(pairs // 2, pairs)(phases)
    hear(2)

    turns = env_bins(0)
    c, s = cos_sin(turns * (float_iota((1, TB), 1) * (DEC * unit)))
    turn_tab[:FB, :] = c
    turn_tab[FB:, :] = -s
    offsets_in.wait()
    for w in range(kept):
        shift = off_ref[w].astype(jnp.float32) * unit
        turn_row[w, :, :FB], turn_row[w, :, FB:] = cos_sin(bins * shift)

    for r in range(3, rounds):
        hear(r)
    own_in.wait()

    def envelope(g):
        at = pl.ds(pl.multiple_of(g * group, group), group)
        mine = own[at].reshape(rows, half).astype(jnp.float32)
        theirs = other[at].reshape(rows, half).astype(jnp.float32)
        a, b = [], []
        for q in range(RADIX // 2):
            cols = slice(q * SPAN, (q + 1) * SPAN)
            a.append(mine[:, cols] + theirs[:, cols])
            b.append(mine[:, cols] - theirs[:, cols])
        s02, d02, s13, d13 = a[0] + a[2], a[0] - a[2], a[1] + a[3], a[1] - a[3]
        t, u = (b[1] - b[3]) * root_half, (b[1] + b[3]) * root_half
        one = (b[0] + t, -(u + b[2]))
        three = (b[0] - t, b[2] - u)
        parts = [
            (s02 + s13, None), one, (d02, -d13), three,
            (s02 - s13, None), (three[0], -three[1]), (d02, d13), (one[0], -one[1]),
        ]
        stacked = []
        for r, (re, im) in enumerate(parts):
            if r == 0:
                zr, zi = re, jnp.zeros_like(re)
            else:
                c, s = fwd_c[r : r + 1, :], fwd_s[r : r + 1, :]
                if im is None:
                    zr, zi = re * c, -(re * s)
                else:
                    zr, zi = re * c + im * s, im * c - re * s
            stacked.append(jnp.concatenate([zr, zi], axis=1).astype(jnp.bfloat16))
        spectrum = jnp.dot(
            jnp.concatenate(stacked, axis=0), fwd[...], preferred_element_type=jnp.float32
        )
        spectrum = spectrum[:, : 2 * BINS] + spectrum[:, 2 * BINS :]
        tapered = []
        for r in range(RADIX):
            high, low = split(spectrum[r * rows : (r + 1) * rows] * gain[r : r + 1, :])
            tapered.append(jnp.concatenate([high, low], axis=1))
        inner = jnp.dot(jnp.concatenate(tapered, axis=0), inv[...], preferred_element_type=jnp.float32)
        turned = []
        for r in range(RADIX):
            re = inner[r * rows : (r + 1) * rows, :INNER]
            im = inner[r * rows : (r + 1) * rows, INNER:]
            if r:
                c, s = inv_c[r : r + 1, :], inv_s[r : r + 1, :]
                re, im = re * c - im * s, re * s + im * c
            turned.append((re, im))
        evens, odds = inverse_four(turned[0::2]), inverse_four(turned[1::2])
        same, cross = [], []
        for q in range(RADIX // 2):
            (er, ei), (fr, fi) = evens[q], odds[q]
            same.append((er * er + ei * ei) + (fr * fr + fi * fi))
            if q == 0:
                both = 2.0 * (er * fr + ei * fi)
            elif q == 1:
                both = (2.0 * root_half) * (er * (fr - fi) + ei * (fr + fi))
            elif q == 2:
                both = 2.0 * (ei * fr - er * fi)
            else:
                both = (2.0 * root_half) * (ei * (fr - fi) - er * (fr + fi))
            cross.append(both)
        total = jnp.sum((same[0] + same[1]) + (same[2] + same[3]), axis=1, keepdims=True)
        even = jnp.dot(
            jnp.concatenate(same, axis=1).astype(jnp.bfloat16), env[0], preferred_element_type=jnp.float32
        )
        odd = jnp.dot(
            jnp.concatenate(cross, axis=1).astype(jnp.bfloat16), env[1], preferred_element_type=jnp.float32
        )
        factor = 4.0 / (math.sqrt(SAMPLES) * (total * (4.0 / SAMPLES) + epsilon))
        even, odd = even * factor, odd * factor
        lower = lax.broadcasted_iota(jnp.int32, (1, FB), 1) < HALF_FB
        e_tab[:, :FB] = jnp.where(lower, even, pltpu.roll(odd, HALF_FB, 1))
        e_tab[:, FB:] = jnp.where(lower, pltpu.roll(even, HALF_FB, 1), odd)

    def outgoing(dest):
        return pltpu.make_async_remote_copy(
            src_ref=send_buf.at[dest],
            dst_ref=recv_buf.at[me],
            send_sem=send_sem,
            recv_sem=recv_sem.at[me],
            device_id={"chan": dest},
            device_id_type=MESH,
        )

    upper = (me // PAIR) // (pairs // 2)

    def pair_at(step):
        return upper * step + (1 - upper) * (pairs - 1 - step)

    def send_pair(step):
        for side in range(PAIR):
            dest = pair_at(step) * PAIR + side

            @pl.when(dest != me)
            def _():
                outgoing(dest).start()

    def stack_up(g, pair):
        at = pl.ds(pl.multiple_of(pair * block, block), block)
        sums = [[acc[pair, p * kept + w] for w in range(kept)] for p in range(2)]
        for ch in range(group):
            pc = phase_c[g * group + ch, at, :]
            ps = phase_s[g * group + ch, at, :]
            for w in range(kept):
                r = kept * ch + w
                er, ei = e_tab[r : r + 1, :FB], e_tab[r : r + 1, FB:]
                sums[0][w] = sums[0][w] + (pc * er - ps * ei)
                sums[1][w] = sums[1][w] + (pc * ei + ps * er)
        return sums

    @pl.loop(0, CHUNKS)
    def _(g):
        exchange(g * group, group, g).wait_recv()
        envelope(g)

        @pl.when(g < CHUNKS - 1)
        def _():
            @pl.loop(0, pairs)
            def _(pair):
                sums = stack_up(g, pair)
                for p in range(2):
                    for w in range(kept):
                        acc[pair, p * kept + w] = sums[p][w]

        @pl.when(g == CHUNKS - 1)
        def _():
            @pl.loop(0, pairs)
            def _(step):
                pair = pair_at(step)
                sums = stack_up(g, pair)
                for side in range(PAIR):
                    part = slice(side * node_rows, (side + 1) * node_rows)
                    packed = jnp.concatenate([sums[p][w][part] for p in range(2) for w in range(kept)], axis=0)
                    send_buf[pair * PAIR + side] = packed.astype(jnp.bfloat16)

                @pl.when(step > 0)
                def _():
                    send_pair(step - 1)

    send_pair(pairs - 1)

    def incoming(source):
        return pltpu.make_async_remote_copy(
            src_ref=send_buf.at[source],
            dst_ref=recv_buf.at[source],
            send_sem=send_sem,
            recv_sem=recv_sem.at[source],
            device_id={"chan": source},
            device_id_type=MESH,
        )

    def add_one(step, stack):
        source = lax.rem(me + step, n_chan)
        incoming(source).wait_recv()
        return stack + recv_buf[source].astype(jnp.float32)

    stack = lax.fori_loop(1, n_chan, add_one, send_buf[me].astype(jnp.float32))

    turned = []
    for w in range(kept):
        c, s = turn_row[w, :, :FB], turn_row[w, :, FB:]
        re = stack[w * node_rows : (w + 1) * node_rows]
        im = stack[(kept + w) * node_rows : (kept + w + 1) * node_rows]
        turned.append(jnp.concatenate([re * c - im * s, re * s + im * c], axis=1))
    bright = jnp.dot(
        jnp.concatenate(turned, axis=0), turn_tab[...],
        precision=lax.Precision.HIGHEST, preferred_element_type=jnp.float32,
    )
    scale = 1.0 / math.sqrt(FB * chans * n_chan)
    out_ref[...] = (bright * scale).reshape(kept, node_rows, TB)

    exchange(0, chans, 0).wait_send()
    pltpu.make_async_remote_copy(
        src_ref=send_buf.at[pl.ds(0, n_chan - 1)],
        dst_ref=recv_buf.at[pl.ds(0, n_chan - 1)],
        send_sem=send_sem,
        recv_sem=recv_sem.at[0],
        device_id={"chan": flip(me, 0)},
        device_id_type=MESH,
    ).wait_send()


def solution(mesh):
    n_chan = mesh.shape["chan"]

    def on_device(traces, delays, offsets):
        chans, windows, half = traces.shape
        nodes = delays.shape[0]
        kept = offsets.shape[0]
        node_rows = nodes // n_chan
        block = PAIR * node_rows
        packed_rows = 2 * kept * node_rows
        hbm = pl.BlockSpec(memory_space=pltpu.HBM)
        return pl.pallas_call(
            functools.partial(kernel, n_chan),
            out_shape=jax.ShapeDtypeStruct((kept, node_rows, TB), jnp.float32),
            in_specs=[hbm] * 3,
            out_specs=pl.BlockSpec(memory_space=pltpu.VMEM),
            scratch_shapes=[
                pltpu.VMEM((chans, nodes), jnp.int32),
                pltpu.VMEM((chans, kept, half), jnp.bfloat16),
                pltpu.VMEM((chans, kept, half), jnp.bfloat16),
                pltpu.VMEM((2 * SPAN, 4 * BINS), jnp.bfloat16),
                pltpu.VMEM((4 * BINS, 2 * INNER), jnp.bfloat16),
                pltpu.VMEM((2, FOLD, FB), jnp.bfloat16),
                pltpu.VMEM((RADIX, SPAN), jnp.float32),
                pltpu.VMEM((RADIX, SPAN), jnp.float32),
                pltpu.VMEM((RADIX, INNER), jnp.float32),
                pltpu.VMEM((RADIX, INNER), jnp.float32),
                pltpu.VMEM((RADIX, 2 * BINS), jnp.float32),
                pltpu.VMEM((chans, nodes, FB), jnp.float32),
                pltpu.VMEM((chans, nodes, FB), jnp.float32),
                pltpu.VMEM((nodes, chans), jnp.float32),
                pltpu.VMEM((2 * FB, TB), jnp.float32),
                pltpu.VMEM((kept, 1, 2 * FB), jnp.float32),
                pltpu.VMEM((kept * chans // CHUNKS, 2 * FB), jnp.float32),
                pltpu.VMEM((n_chan // PAIR, 2 * kept, block, FB), jnp.float32),
                pltpu.VMEM((n_chan, packed_rows, FB), jnp.bfloat16),
                pltpu.VMEM((n_chan, packed_rows, FB), jnp.bfloat16),
                pltpu.SMEM((kept,), jnp.int32),
                pltpu.SemaphoreType.DMA,
                pltpu.SemaphoreType.DMA,
                pltpu.SemaphoreType.DMA,
                pltpu.SemaphoreType.DMA,
                pltpu.SemaphoreType.DMA((CHUNKS,)),
                pltpu.SemaphoreType.DMA,
                pltpu.SemaphoreType.DMA((n_chan,)),
                pltpu.SemaphoreType.REGULAR((n_chan.bit_length() - 1,)),
            ],
            compiler_params=pltpu.CompilerParams(
                collective_id=0, has_side_effects=True, vmem_limit_bytes=16 * 1024 * 1024 + 8 * chans * nodes * FB
            ),
        )(*(pltpu.with_memory_space_constraint(a, pltpu.HBM) for a in (traces, delays.T, offsets)))

    placed = (P("chan", None, "tm"), P(None, "chan"), P("tm"))
    return jax.shard_map(
        on_device, mesh=mesh, in_specs=placed, out_specs=P("tm", "chan", None), check_vma=False
    )
```

time: 19.1 us -> 18.9 us (0.990)
  local copies, waits for them, and re-layouts: 1.64 us -> 0.61 us
  Pallas kernels: 17.4 us -> 18.1 us
    unnamed x2 -> x1, local copies, waits for them, and re-layouts: 1.64 us -> 0.61 us
    pallas_call x1, Pallas kernels: 17.4 us -> 18.1 us  [on_device(): pl.pallas_call(functools.partial(kernel, n_chan), out_shape=jax.ShapeDtyp...]
where the time goes in v1:
time: 18.9 us; the launch traced here: 18.7 us
  Pallas kernels  18.1 us (96%)
  local copies, waits for them, and re-layouts  0.61 us (3%)
    pallas_call x1, Pallas kernels, on_device(): pl.pallas_call(functools.partial(kernel, n_chan), out_shape=jax.ShapeDtyp...  18.1 us
    unnamed x1, local copies, waits for them, and re-layouts  0.61 us

profile of v1, /device:TPU:0, one launch (start us, length us, event | category | flops | bytes accessed | tf_op | source)
XLA Modules:
  0.0 18.7 jit_solution(3440038861917030100)
XLA Ops:
  0.0 18.1 %shard_map.37 = f32[2,8,256]{2,1,0:T(8,128)S(1)} custom-call(bf16[32,4,1024]{2,1,0:T(4,128)(2,1)} %x_hbm.1, s32[32,128]{1,0:T(8,128)} %bitcast.1, s32[2]{0:T(128)} %off_hbm.1), custom_call_target="tpu_custom_call" | custom-call | tf_op jit(solution)/shard_map/pallas_call | solution.py:408
  18.1 0.6 %copy.5 = f32[2,8,256]{2,1,0:T(8,128)} copy(f32[2,8,256]{2,1,0:T(8,128)S(1)} %shard_map.37) | data formatting | bytes 32768

commit v2 on v1

--- a/solution.py
+++ b/solution.py
@@ -15,7 +15,8 @@
 BAND_LO = 128
 DEC = 8
 PAIR = 2
-CHUNKS = 4
+CHUNKS = 2
+EARLY = 2
 
 RADIX = 8
 SPAN = SAMPLES // RADIX
@@ -31,24 +32,22 @@
 MESH = pl.DeviceIdType.MESH
 
 
-COS_TURN = (
-    0.9999999890590201, -19.739204499453688, 64.93911745988827, -85.45013953077586,
-    60.16763095018129, -25.96759924584206, 6.528658157862129,
+COS_HALF = (
+    1.4142134965650053, -6.978850988237948, 5.73946117066148, -1.8835629871727047, 0.3106981915530425,
 )
-SIN_TURN = (
-    6.283185302511498, -41.341700405316736, 81.60513138576982, -76.70301535347629,
-    42.02592698341473, -14.899846660399582, 3.2381375010236435,
+SIN_HALF = (
+    4.442882834149914, -7.30824115454536, 3.6062889582107696, -0.845763596066154, 0.10920575349257165,
 )
 
 
 def cos_sin(turns):
     x = turns - jnp.round(turns)
     y = x * x
-    c, s = COS_TURN[-1], SIN_TURN[-1]
-    for c_next, s_next in zip(COS_TURN[-2::-1], SIN_TURN[-2::-1]):
+    c, s = COS_HALF[-1], SIN_HALF[-1]
+    for c_next, s_next in zip(COS_HALF[-2::-1], SIN_HALF[-2::-1]):
         c = c * y + c_next
         s = s * y + s_next
-    return c, s * x
+    return c * c - 1.0, s * x * c
 
 
 def float_iota(shape, axis):
@@ -155,8 +154,8 @@
         c, s = cos_sin(spot * ((place + BAND_LO // RADIX) * (1.0 / SPAN)) + quarter)
         for value, base in ((c, 0), (s, SPAN)):
             high, low = split(value)
-            fwd[pl.ds(pl.multiple_of(base + first, 32), 32), : 2 * BINS] = high
-            fwd[pl.ds(pl.multiple_of(base + first, 32), 32), 2 * BINS :] = low
+            fwd[0, pl.ds(pl.multiple_of(base + first, 32), 32), :] = high
+            fwd[1, pl.ds(pl.multiple_of(base + first, 32), 32), :] = low
 
     pl.loop(0, SPAN // 32)(forward_table)
 
@@ -165,8 +164,8 @@
     row_place = jnp.where(row < BINS, row, row - BINS).astype(jnp.float32)
     c, s = cos_sin(row_place * (float_iota((1, INNER), 1) * (1.0 / INNER)) + row_quarter)
     for base in (0, 2 * BINS):
-        inv[base : base + 2 * BINS, :INNER] = c.astype(jnp.bfloat16)
-        inv[base : base + 2 * BINS, INNER:] = s.astype(jnp.bfloat16)
+        inv[0, base : base + 2 * BINS, :] = c.astype(jnp.bfloat16)
+        inv[1, base : base + 2 * BINS, :] = s.astype(jnp.bfloat16)
 
     env_lane = lax.broadcasted_iota(jnp.int32, (1, FB), 1)
     env_quarter = jnp.where(env_lane < HALF_FB, 0.0, 0.25)
@@ -194,11 +193,14 @@
             c, s = cos_sin(delay[:, ch : ch + 1] * bins)
             phase_c[ch, at, :] = c
             phase_s[ch, at, :] = s
-        acc[step] = jnp.zeros(acc.shape[1:], jnp.float32)
-
-    pl.loop(0, pairs // 2)(phases)
+
+    def two_phases(step):
+        phases(2 * step)
+        phases(2 * step + 1)
+
+    pl.loop(0, pairs // 4)(two_phases)
     hear(1)
-    pl.loop(pairs // 2, pairs)(phases)
+    pl.loop(pairs // 4, pairs // 2)(two_phases)
     hear(2)
 
     turns = env_bins(0)
@@ -210,8 +212,6 @@
         shift = off_ref[w].astype(jnp.float32) * unit
         turn_row[w, :, :FB], turn_row[w, :, FB:] = cos_sin(bins * shift)
 
-    for r in range(3, rounds):
-        hear(r)
     own_in.wait()
 
     def envelope(g):
@@ -243,14 +243,14 @@
                     zr, zi = re * c + im * s, im * c - re * s
             stacked.append(jnp.concatenate([zr, zi], axis=1).astype(jnp.bfloat16))
         spectrum = jnp.dot(
-            jnp.concatenate(stacked, axis=0), fwd[...], preferred_element_type=jnp.float32
+            jnp.concatenate(stacked, axis=0), jnp.concatenate([fwd[0], fwd[1]], axis=1), preferred_element_type=jnp.float32
         )
         spectrum = spectrum[:, : 2 * BINS] + spectrum[:, 2 * BINS :]
         tapered = []
         for r in range(RADIX):
             high, low = split(spectrum[r * rows : (r + 1) * rows] * gain[r : r + 1, :])
             tapered.append(jnp.concatenate([high, low], axis=1))
-        inner = jnp.dot(jnp.concatenate(tapered, axis=0), inv[...], preferred_element_type=jnp.float32)
+        inner = jnp.dot(jnp.concatenate(tapered, axis=0), jnp.concatenate([inv[0], inv[1]], axis=1), preferred_element_type=jnp.float32)
         turned = []
         for r in range(RADIX):
             re = inner[r * rows : (r + 1) * rows, :INNER]
@@ -283,8 +283,8 @@
         factor = 4.0 / (math.sqrt(SAMPLES) * (total * (4.0 / SAMPLES) + epsilon))
         even, odd = even * factor, odd * factor
         lower = lax.broadcasted_iota(jnp.int32, (1, FB), 1) < HALF_FB
-        e_tab[:, :FB] = jnp.where(lower, even, pltpu.roll(odd, HALF_FB, 1))
-        e_tab[:, FB:] = jnp.where(lower, pltpu.roll(even, HALF_FB, 1), odd)
+        e_tab[g, :, :FB] = jnp.where(lower, even, pltpu.roll(odd, HALF_FB, 1))
+        e_tab[g, :, FB:] = jnp.where(lower, pltpu.roll(even, HALF_FB, 1), odd)
 
     def outgoing(dest):
         return pltpu.make_async_remote_copy(
@@ -309,47 +309,53 @@
             def _():
                 outgoing(dest).start()
 
-    def stack_up(g, pair):
+    def stack_up(g, pair, sums):
         at = pl.ds(pl.multiple_of(pair * block, block), block)
-        sums = [[acc[pair, p * kept + w] for w in range(kept)] for p in range(2)]
         for ch in range(group):
             pc = phase_c[g * group + ch, at, :]
             ps = phase_s[g * group + ch, at, :]
             for w in range(kept):
                 r = kept * ch + w
-                er, ei = e_tab[r : r + 1, :FB], e_tab[r : r + 1, FB:]
+                er, ei = e_tab[g, r : r + 1, :FB], e_tab[g, r : r + 1, FB:]
                 sums[0][w] = sums[0][w] + (pc * er - ps * ei)
                 sums[1][w] = sums[1][w] + (pc * ei + ps * er)
         return sums
+
+    def pack(pair, sums):
+        for side in range(PAIR):
+            part = slice(side * node_rows, (side + 1) * node_rows)
+            packed = jnp.concatenate([sums[p][w][part] for p in range(2) for w in range(kept)], axis=0)
+            send_buf[pair * PAIR + side] = packed.astype(jnp.bfloat16)
+
+    acc[...] = jnp.zeros_like(acc)
 
     @pl.loop(0, CHUNKS)
     def _(g):
         exchange(g * group, group, g).wait_recv()
         envelope(g)
-
-        @pl.when(g < CHUNKS - 1)
-        def _():
-            @pl.loop(0, pairs)
-            def _(pair):
-                sums = stack_up(g, pair)
-                for p in range(2):
-                    for w in range(kept):
-                        acc[pair, p * kept + w] = sums[p][w]
-
-        @pl.when(g == CHUNKS - 1)
-        def _():
-            @pl.loop(0, pairs)
-            def _(step):
-                pair = pair_at(step)
-                sums = stack_up(g, pair)
-                for side in range(PAIR):
-                    part = slice(side * node_rows, (side + 1) * node_rows)
-                    packed = jnp.concatenate([sums[p][w][part] for p in range(2) for w in range(kept)], axis=0)
-                    send_buf[pair * PAIR + side] = packed.astype(jnp.bfloat16)
-
-                @pl.when(step > 0)
-                def _():
+        for step in range(EARLY):
+            pair = pair_at(step)
+            sums = stack_up(g, pair, [[acc[step, p * kept + w] for w in range(kept)] for p in range(2)])
+            for p in range(2):
+                for w in range(kept):
+                    acc[step, p * kept + w] = sums[p][w]
+
+            @pl.when(g == CHUNKS - 1)
+            def _():
+                pack(pair, sums)
+                if step:
+                    for r in range(3, rounds):
+                        hear(r)
                     send_pair(step - 1)
+
+    @pl.loop(EARLY, pairs)
+    def _(step):
+        pair = pair_at(step)
+        sums = [[jnp.zeros((block, FB), jnp.float32) for _ in range(kept)] for _ in range(2)]
+        for g in range(CHUNKS):
+            sums = stack_up(g, pair, sums)
+        pack(pair, sums)
+        send_pair(step - 1)
 
     send_pair(pairs - 1)
 
@@ -414,8 +420,8 @@
                 pltpu.VMEM((chans, nodes), jnp.int32),
                 pltpu.VMEM((chans, kept, half), jnp.bfloat16),
                 pltpu.VMEM((chans, kept, half), jnp.bfloat16),
-                pltpu.VMEM((2 * SPAN, 4 * BINS), jnp.bfloat16),
-                pltpu.VMEM((4 * BINS, 2 * INNER), jnp.bfloat16),
+                pltpu.VMEM((2, 2 * SPAN, 2 * BINS), jnp.bfloat16),
+                pltpu.VMEM((2, 4 * BINS, INNER), jnp.bfloat16),
                 pltpu.VMEM((2, FOLD, FB), jnp.bfloat16),
                 pltpu.VMEM((RADIX, SPAN), jnp.float32),
                 pltpu.VMEM((RADIX, SPAN), jnp.float32),
@@ -427,8 +433,8 @@
                 pltpu.VMEM((nodes, chans), jnp.float32),
                 pltpu.VMEM((2 * FB, TB), jnp.float32),
                 pltpu.VMEM((kept, 1, 2 * FB), jnp.float32),
-                pltpu.VMEM((kept * chans // CHUNKS, 2 * FB), jnp.float32),
-                pltpu.VMEM((n_chan // PAIR, 2 * kept, block, FB), jnp.float32),
+                pltpu.VMEM((CHUNKS, kept * chans // CHUNKS, 2 * FB), jnp.float32),
+                pltpu.VMEM((EARLY, 2 * kept, block, FB), jnp.float32),
                 pltpu.VMEM((n_chan, packed_rows, FB), jnp.bfloat16),
                 pltpu.VMEM((n_chan, packed_rows, FB), jnp.bfloat16),
                 pltpu.SMEM((kept,), jnp.int32),

time: 18.9 us -> 16.9 us (0.89)
  Pallas kernels: 18.1 us -> 16.2 us
    pallas_call x1, Pallas kernels: 18.1 us -> 16.2 us  [on_device(): pl.pallas_call(functools.partial(kernel, n_chan), out_shape=jax.ShapeDtyp...]
where the time goes in v2:
time: 16.9 us; the launch traced here: 16.8 us
  Pallas kernels  16.2 us (96%)
  local copies, waits for them, and re-layouts  0.61 us (4%)
    pallas_call x1, Pallas kernels, on_device(): pl.pallas_call(functools.partial(kernel, n_chan), out_shape=jax.ShapeDtyp...  16.2 us
    unnamed x1, local copies, waits for them, and re-layouts  0.61 us

profile of v2, /device:TPU:0, one launch (start us, length us, event | category | flops | bytes accessed | tf_op | source)
XLA Modules:
  0.0 16.8 jit_solution(3078761614870382037)
XLA Ops:
  0.0 16.2 %shard_map.37 = f32[2,8,256]{2,1,0:T(8,128)S(1)} custom-call(bf16[32,4,1024]{2,1,0:T(4,128)(2,1)} %x_hbm.1, s32[32,128]{1,0:T(8,128)} %bitcast.1, s32[2]{0:T(128)} %off_hbm.1), custom_call_target="tpu_custom_call" | custom-call | tf_op jit(solution)/shard_map/pallas_call | solution.py:414
  16.2 0.6 %copy.5 = f32[2,8,256]{2,1,0:T(8,128)} copy(f32[2,8,256]{2,1,0:T(8,128)S(1)} %shard_map.37) | data formatting | bytes 32768

commit v3 on v2

--- a/solution.py
+++ b/solution.py
@@ -86,10 +86,11 @@
     nodes_d, turn_tab, turn_row, e_tab, acc, send_buf, recv_buf,
     off_ref, off_sem, d_sem, x_in, x_send, x_recv, send_sem, recv_sem, round_sem,
 ):
-    chans, kept, half = own.shape
+    chans, nodes = d_ref.shape
+    half = own.shape[1]
+    kept = own.shape[0] // chans
     group = chans // CHUNKS
     rows = kept * group
-    nodes = d_hbm.shape[1]
     node_rows = nodes // n_chan
     me = lax.axis_index("chan")
     tm = lax.axis_index("tm")
@@ -104,12 +105,8 @@
 
     offsets_in = pltpu.make_async_copy(off_hbm, off_ref, off_sem)
     delays_in = pltpu.make_async_copy(d_hbm, d_ref, d_sem)
-    own_in = pltpu.make_async_copy(
-        x_hbm.at[:, pl.ds(pl.multiple_of(tm * kept, kept), kept)], own, x_in
-    )
     delays_in.start()
     offsets_in.start()
-    own_in.start()
 
     def tell(r):
         if r < rounds:
@@ -120,20 +117,26 @@
             pl.semaphore_wait(round_sem.at[r], 1)
             tell(r + 1)
 
-    def exchange(first, count, at):
+    def mine_of(ch):
+        return pltpu.make_async_copy(
+            x_hbm.at[ch, pl.ds(pl.multiple_of(tm * kept, kept), kept)], own.at[pl.ds(ch * kept, kept)], x_in
+        )
+
+    def to_partner(src, dst, at):
         return pltpu.make_async_remote_copy(
-            src_ref=x_hbm.at[pl.ds(first, count), pl.ds(pl.multiple_of(partner * kept, kept), kept)],
-            dst_ref=other.at[pl.ds(first, count)],
-            send_sem=x_send,
-            recv_sem=x_recv.at[at],
-            device_id={"tm": partner},
-            device_id_type=MESH,
+            src_ref=src, dst_ref=dst, send_sem=x_send, recv_sem=x_recv.at[at],
+            device_id={"tm": partner}, device_id_type=MESH,
         )
 
     pl.semaphore_wait(barrier, rounds + 1)
-    for g in range(CHUNKS):
-        exchange(g * group, group, g).start()
+    for ch in range(chans):
+        to_partner(
+            x_hbm.at[ch, pl.ds(pl.multiple_of(partner * kept, kept), kept)],
+            other.at[pl.ds(ch * kept, kept)], ch // group,
+        ).start()
     tell(0)
+    for ch in range(chans):
+        mine_of(ch).start()
 
     late = jnp.where(lax.broadcasted_iota(jnp.int32, (1, SPAN), 1) * 0 + tm == 1, -1.0, 1.0)
     residue = lax.broadcasted_iota(jnp.int32, (RADIX, SPAN), 0)
@@ -205,19 +208,20 @@
 
     turns = env_bins(0)
     c, s = cos_sin(turns * (float_iota((1, TB), 1) * (DEC * unit)))
-    turn_tab[:FB, :] = c
-    turn_tab[FB:, :] = -s
+    for first, value in ((0, c), (FB, -s)):
+        for piece, part in enumerate(split(value)):
+            turn_tab[first : first + FB, piece * TB : (piece + 1) * TB] = part
     offsets_in.wait()
     for w in range(kept):
         shift = off_ref[w].astype(jnp.float32) * unit
         turn_row[w, :, :FB], turn_row[w, :, FB:] = cos_sin(bins * shift)
 
-    own_in.wait()
+    pltpu.make_async_copy(own, own, x_in).wait()
 
     def envelope(g):
-        at = pl.ds(pl.multiple_of(g * group, group), group)
-        mine = own[at].reshape(rows, half).astype(jnp.float32)
-        theirs = other[at].reshape(rows, half).astype(jnp.float32)
+        at = pl.ds(pl.multiple_of(g * rows, rows), rows)
+        mine = own[at, :].astype(jnp.float32)
+        theirs = other[at, :].astype(jnp.float32)
         a, b = [], []
         for q in range(RADIX // 2):
             cols = slice(q * SPAN, (q + 1) * SPAN)
@@ -296,14 +300,9 @@
             device_id_type=MESH,
         )
 
-    upper = (me // PAIR) // (pairs // 2)
-
-    def pair_at(step):
-        return upper * step + (1 - upper) * (pairs - 1 - step)
-
-    def send_pair(step):
+    def send_pair(pair):
         for side in range(PAIR):
-            dest = pair_at(step) * PAIR + side
+            dest = pair * PAIR + side
 
             @pl.when(dest != me)
             def _():
@@ -331,18 +330,18 @@
 
     @pl.loop(0, CHUNKS)
     def _(g):
-        exchange(g * group, group, g).wait_recv()
+        arrived = other.at[pl.ds(pl.multiple_of(g * rows, rows), rows)]
+        to_partner(arrived, arrived, g).wait_recv()
         envelope(g)
         for step in range(EARLY):
-            pair = pair_at(step)
-            sums = stack_up(g, pair, [[acc[step, p * kept + w] for w in range(kept)] for p in range(2)])
+            sums = stack_up(g, step, [[acc[step, p * kept + w] for w in range(kept)] for p in range(2)])
             for p in range(2):
                 for w in range(kept):
                     acc[step, p * kept + w] = sums[p][w]
 
             @pl.when(g == CHUNKS - 1)
             def _():
-                pack(pair, sums)
+                pack(step, sums)
                 if step:
                     for r in range(3, rounds):
                         hear(r)
@@ -350,11 +349,10 @@
 
     @pl.loop(EARLY, pairs)
     def _(step):
-        pair = pair_at(step)
         sums = [[jnp.zeros((block, FB), jnp.float32) for _ in range(kept)] for _ in range(2)]
         for g in range(CHUNKS):
-            sums = stack_up(g, pair, sums)
-        pack(pair, sums)
+            sums = stack_up(g, step, sums)
+        pack(step, sums)
         send_pair(step - 1)
 
     send_pair(pairs - 1)
@@ -382,14 +380,16 @@
         re = stack[w * node_rows : (w + 1) * node_rows]
         im = stack[(kept + w) * node_rows : (kept + w + 1) * node_rows]
         turned.append(jnp.concatenate([re * c - im * s, re * s + im * c], axis=1))
+    high, low = split(jnp.concatenate(turned, axis=0))
     bright = jnp.dot(
-        jnp.concatenate(turned, axis=0), turn_tab[...],
-        precision=lax.Precision.HIGHEST, preferred_element_type=jnp.float32,
+        jnp.concatenate([high, low], axis=0), turn_tab[...], preferred_element_type=jnp.float32
     )
+    size = kept * node_rows
+    bright = bright[:size, :TB] + (bright[:size, TB:] + bright[size:, :TB])
     scale = 1.0 / math.sqrt(FB * chans * n_chan)
     out_ref[...] = (bright * scale).reshape(kept, node_rows, TB)
 
-    exchange(0, chans, 0).wait_send()
+    to_partner(other, other, 0).wait_send()
     pltpu.make_async_remote_copy(
         src_ref=send_buf.at[pl.ds(0, n_chan - 1)],
         dst_ref=recv_buf.at[pl.ds(0, n_chan - 1)],
@@ -418,8 +418,8 @@
             out_specs=pl.BlockSpec(memory_space=pltpu.VMEM),
             scratch_shapes=[
                 pltpu.VMEM((chans, nodes), jnp.int32),
-                pltpu.VMEM((chans, kept, half), jnp.bfloat16),
-                pltpu.VMEM((chans, kept, half), jnp.bfloat16),
+                pltpu.VMEM((chans * kept, half), jnp.bfloat16),
+                pltpu.VMEM((chans * kept, half), jnp.bfloat16),
                 pltpu.VMEM((2, 2 * SPAN, 2 * BINS), jnp.bfloat16),
                 pltpu.VMEM((2, 4 * BINS, INNER), jnp.bfloat16),
                 pltpu.VMEM((2, FOLD, FB), jnp.bfloat16),
@@ -431,7 +431,7 @@
                 pltpu.VMEM((chans, nodes, FB), jnp.float32),
                 pltpu.VMEM((chans, nodes, FB), jnp.float32),
                 pltpu.VMEM((nodes, chans), jnp.float32),
-                pltpu.VMEM((2 * FB, TB), jnp.float32),
+                pltpu.VMEM((2 * FB, 2 * TB), jnp.bfloat16),
                 pltpu.VMEM((kept, 1, 2 * FB), jnp.float32),
                 pltpu.VMEM((CHUNKS, kept * chans // CHUNKS, 2 * FB), jnp.float32),
                 pltpu.VMEM((EARLY, 2 * kept, block, FB), jnp.float32),

time: 16.9 us -> 15.8 us (0.935)
  Pallas kernels: 16.2 us -> 15.1 us
    pallas_call x1, Pallas kernels: 16.2 us -> 15.1 us  [on_device(): pl.pallas_call(functools.partial(kernel, n_chan), out_shape=jax.ShapeDtyp...]
where the time goes in v3:
time: 15.8 us; the launch traced here: 15.7 us
  Pallas kernels  15.1 us (96%)
  local copies, waits for them, and re-layouts  0.61 us (4%)
    pallas_call x1, Pallas kernels, on_device(): pl.pallas_call(functools.partial(kernel, n_chan), out_shape=jax.ShapeDtyp...  15.1 us
    unnamed x1, local copies, waits for them, and re-layouts  0.61 us

profile of v3, /device:TPU:0, one launch (start us, length us, event | category | flops | bytes accessed | tf_op | source)
XLA Modules:
  0.0 15.7 jit_solution(15582750401680085854)
XLA Ops:
  0.0 15.1 %shard_map.37 = f32[2,8,256]{2,1,0:T(8,128)S(1)} custom-call(bf16[32,4,1024]{2,1,0:T(4,128)(2,1)} %x_hbm.1, s32[32,128]{1,0:T(8,128)} %bitcast.1, s32[2]{0:T(128)} %off_hbm.1), custom_call_target="tpu_custom_call" | custom-call | tf_op jit(solution)/shard_map/pallas_call | solution.py:414
  15.1 0.6 %copy.5 = f32[2,8,256]{2,1,0:T(8,128)} copy(f32[2,8,256]{2,1,0:T(8,128)S(1)} %shard_map.37) | data formatting | bytes 32768

commit v4 on v3

--- a/solution.py
+++ b/solution.py
@@ -14,7 +14,7 @@
 TB = 256
 BAND_LO = 128
 DEC = 8
-PAIR = 2
+UNROLL = 4
 CHUNKS = 2
 EARLY = 2
 
@@ -156,9 +156,7 @@
         spot = float_iota((32, 2 * BINS), 0) + first.astype(jnp.float32)
         c, s = cos_sin(spot * ((place + BAND_LO // RADIX) * (1.0 / SPAN)) + quarter)
         for value, base in ((c, 0), (s, SPAN)):
-            high, low = split(value)
-            fwd[0, pl.ds(pl.multiple_of(base + first, 32), 32), :] = high
-            fwd[1, pl.ds(pl.multiple_of(base + first, 32), 32), :] = low
+            fwd[pl.ds(pl.multiple_of(base + first, 32), 32), :] = value.astype(jnp.bfloat16)
 
     pl.loop(0, SPAN // 32)(forward_table)
 
@@ -171,39 +169,41 @@
         inv[1, base : base + 2 * BINS, :] = s.astype(jnp.bfloat16)
 
     env_lane = lax.broadcasted_iota(jnp.int32, (1, FB), 1)
-    env_quarter = jnp.where(env_lane < HALF_FB, 0.0, 0.25)
     env_place = jnp.where(env_lane < HALF_FB, env_lane, env_lane - HALF_FB).astype(jnp.float32)
     for odd in range(2):
         freq = (2.0 * env_place + (1.0 if odd else 2.0)) * (1.0 / TIMES)
-        base_c, base_s = cos_sin(float_iota((32, FB), 0) * freq + env_quarter)
+        base_c, base_s = cos_sin(float_iota((32, FB), 0) * freq)
         lead_c, lead_s = cos_sin(float_iota((FOLD // 32, FB), 0) * (freq * 32.0))
+        shown = (env_lane >= HALF_FB) == bool(odd)
+        base_c, base_s = jnp.where(shown, base_c, 0.0), jnp.where(shown, base_s, 0.0)
         for a in range(FOLD // 32):
-            value = lead_c[a : a + 1] * base_c - lead_s[a : a + 1] * base_s
-            env[odd, a * 32 : (a + 1) * 32, :] = value.astype(jnp.bfloat16)
+            lc, ls = lead_c[a : a + 1], lead_s[a : a + 1]
+            at = slice(odd * FOLD + a * 32, odd * FOLD + (a + 1) * 32)
+            env[0, at, :] = (lc * base_c - ls * base_s).astype(jnp.bfloat16)
+            env[1, at, :] = -(ls * base_c + lc * base_s).astype(jnp.bfloat16)
 
     hear(0)
 
     delays_in.wait()
     nodes_d[...] = (d_ref[...].astype(jnp.float32) * unit).T
-    block = PAIR * node_rows
     bins = env_bins(1)
-    pairs = n_chan // PAIR
 
     def phases(step):
-        at = pl.ds(pl.multiple_of(step * block, block), block)
+        at = pl.ds(pl.multiple_of(step * node_rows, node_rows), node_rows)
         delay = nodes_d[at, :]
         for ch in range(chans):
             c, s = cos_sin(delay[:, ch : ch + 1] * bins)
             phase_c[ch, at, :] = c
             phase_s[ch, at, :] = s
 
-    def two_phases(step):
-        phases(2 * step)
-        phases(2 * step + 1)
-
-    pl.loop(0, pairs // 4)(two_phases)
+    def more_phases(step):
+        for k in range(UNROLL):
+            phases(UNROLL * step + k)
+
+    steps = n_chan // UNROLL
+    pl.loop(0, steps // 2)(more_phases)
     hear(1)
-    pl.loop(pairs // 4, pairs // 2)(two_phases)
+    pl.loop(steps // 2, steps)(more_phases)
     hear(2)
 
     turns = env_bins(0)
@@ -247,9 +247,8 @@
                     zr, zi = re * c + im * s, im * c - re * s
             stacked.append(jnp.concatenate([zr, zi], axis=1).astype(jnp.bfloat16))
         spectrum = jnp.dot(
-            jnp.concatenate(stacked, axis=0), jnp.concatenate([fwd[0], fwd[1]], axis=1), preferred_element_type=jnp.float32
-        )
-        spectrum = spectrum[:, : 2 * BINS] + spectrum[:, 2 * BINS :]
+            jnp.concatenate(stacked, axis=0), fwd[...], preferred_element_type=jnp.float32
+        )
         tapered = []
         for r in range(RADIX):
             high, low = split(spectrum[r * rows : (r + 1) * rows] * gain[r : r + 1, :])
@@ -278,17 +277,12 @@
                 both = (2.0 * root_half) * (ei * (fr - fi) - er * (fr + fi))
             cross.append(both)
         total = jnp.sum((same[0] + same[1]) + (same[2] + same[3]), axis=1, keepdims=True)
-        even = jnp.dot(
-            jnp.concatenate(same, axis=1).astype(jnp.bfloat16), env[0], preferred_element_type=jnp.float32
-        )
-        odd = jnp.dot(
-            jnp.concatenate(cross, axis=1).astype(jnp.bfloat16), env[1], preferred_element_type=jnp.float32
+        spread = jnp.dot(
+            jnp.concatenate(same + cross, axis=1).astype(jnp.bfloat16),
+            jnp.concatenate([env[0], env[1]], axis=1), preferred_element_type=jnp.float32,
         )
         factor = 4.0 / (math.sqrt(SAMPLES) * (total * (4.0 / SAMPLES) + epsilon))
-        even, odd = even * factor, odd * factor
-        lower = lax.broadcasted_iota(jnp.int32, (1, FB), 1) < HALF_FB
-        e_tab[g, :, :FB] = jnp.where(lower, even, pltpu.roll(odd, HALF_FB, 1))
-        e_tab[g, :, FB:] = jnp.where(lower, pltpu.roll(even, HALF_FB, 1), odd)
+        e_tab[g] = spread * factor
 
     def outgoing(dest):
         return pltpu.make_async_remote_copy(
@@ -300,16 +294,13 @@
             device_id_type=MESH,
         )
 
-    def send_pair(pair):
-        for side in range(PAIR):
-            dest = pair * PAIR + side
-
-            @pl.when(dest != me)
-            def _():
-                outgoing(dest).start()
-
-    def stack_up(g, pair, sums):
-        at = pl.ds(pl.multiple_of(pair * block, block), block)
+    def send(dest):
+        @pl.when(dest != me)
+        def _():
+            outgoing(dest).start()
+
+    def stack_up(g, dest, sums):
+        at = pl.ds(pl.multiple_of(dest * node_rows, node_rows), node_rows)
         for ch in range(group):
             pc = phase_c[g * group + ch, at, :]
             ps = phase_s[g * group + ch, at, :]
@@ -320,11 +311,9 @@
                 sums[1][w] = sums[1][w] + (pc * ei + ps * er)
         return sums
 
-    def pack(pair, sums):
-        for side in range(PAIR):
-            part = slice(side * node_rows, (side + 1) * node_rows)
-            packed = jnp.concatenate([sums[p][w][part] for p in range(2) for w in range(kept)], axis=0)
-            send_buf[pair * PAIR + side] = packed.astype(jnp.bfloat16)
+    def pack(dest, sums):
+        packed = jnp.concatenate([sums[p][w] for p in range(2) for w in range(kept)], axis=0)
+        send_buf[dest] = packed.astype(jnp.bfloat16)
 
     acc[...] = jnp.zeros_like(acc)
 
@@ -342,20 +331,21 @@
             @pl.when(g == CHUNKS - 1)
             def _():
                 pack(step, sums)
-                if step:
+                if step == 1:
                     for r in range(3, rounds):
                         hear(r)
-                    send_pair(step - 1)
-
-    @pl.loop(EARLY, pairs)
+                if step:
+                    send(step - 1)
+
+    @pl.loop(EARLY, n_chan)
     def _(step):
-        sums = [[jnp.zeros((block, FB), jnp.float32) for _ in range(kept)] for _ in range(2)]
+        sums = [[jnp.zeros((node_rows, FB), jnp.float32) for _ in range(kept)] for _ in range(2)]
         for g in range(CHUNKS):
             sums = stack_up(g, step, sums)
         pack(step, sums)
-        send_pair(step - 1)
-
-    send_pair(pairs - 1)
+        send(step - 1)
+
+    send(n_chan - 1)
 
     def incoming(source):
         return pltpu.make_async_remote_copy(
@@ -408,7 +398,6 @@
         nodes = delays.shape[0]
         kept = offsets.shape[0]
         node_rows = nodes // n_chan
-        block = PAIR * node_rows
         packed_rows = 2 * kept * node_rows
         hbm = pl.BlockSpec(memory_space=pltpu.HBM)
         return pl.pallas_call(
@@ -420,9 +409,9 @@
                 pltpu.VMEM((chans, nodes), jnp.int32),
                 pltpu.VMEM((chans * kept, half), jnp.bfloat16),
                 pltpu.VMEM((chans * kept, half), jnp.bfloat16),
-                pltpu.VMEM((2, 2 * SPAN, 2 * BINS), jnp.bfloat16),
+                pltpu.VMEM((2 * SPAN, 2 * BINS), jnp.bfloat16),
                 pltpu.VMEM((2, 4 * BINS, INNER), jnp.bfloat16),
-                pltpu.VMEM((2, FOLD, FB), jnp.bfloat16),
+                pltpu.VMEM((2, TIMES, FB), jnp.bfloat16),
                 pltpu.VMEM((RADIX, SPAN), jnp.float32),
                 pltpu.VMEM((RADIX, SPAN), jnp.float32),
                 pltpu.VMEM((RADIX, INNER), jnp.float32),
@@ -434,7 +423,7 @@
                 pltpu.VMEM((2 * FB, 2 * TB), jnp.bfloat16),
                 pltpu.VMEM((kept, 1, 2 * FB), jnp.float32),
                 pltpu.VMEM((CHUNKS, kept * chans // CHUNKS, 2 * FB), jnp.float32),
-                pltpu.VMEM((EARLY, 2 * kept, block, FB), jnp.float32),
+                pltpu.VMEM((EARLY, 2 * kept, node_rows, FB), jnp.float32),
                 pltpu.VMEM((n_chan, packed_rows, FB), jnp.bfloat16),
                 pltpu.VMEM((n_chan, packed_rows, FB), jnp.bfloat16),
                 pltpu.SMEM((kept,), jnp.int32),

time: 15.8 us -> 15.5 us (0.981)
  Pallas kernels: 15.1 us -> 14.7 us
    pallas_call x1, Pallas kernels: 15.1 us -> 14.7 us  [on_device(): pl.pallas_call(functools.partial(kernel, n_chan), out_shape=jax.ShapeDtyp...]
where the time goes in v4:
time: 15.5 us; the launch traced here: 15.3 us
  Pallas kernels  14.7 us (95%)
  local copies, waits for them, and re-layouts  0.61 us (4%)
    pallas_call x1, Pallas kernels, on_device(): pl.pallas_call(functools.partial(kernel, n_chan), out_shape=jax.ShapeDtyp...  14.7 us
    unnamed x1, local copies, waits for them, and re-layouts  0.61 us

profile of v4, /device:TPU:0, one launch (start us, length us, event | category | flops | bytes accessed | tf_op | source)
XLA Modules:
  0.0 15.3 jit_solution(9967179865022786053)
XLA Ops:
  0.0 14.7 %shard_map.37 = f32[2,8,256]{2,1,0:T(8,128)S(1)} custom-call(bf16[32,4,1024]{2,1,0:T(4,128)(2,1)} %x_hbm.1, s32[32,128]{1,0:T(8,128)} %bitcast.1, s32[2]{0:T(128)} %off_hbm.1), custom_call_target="tpu_custom_call" | custom-call | tf_op jit(solution)/shard_map/pallas_call | solution.py:403
  14.7 0.6 %copy.5 = f32[2,8,256]{2,1,0:T(8,128)} copy(f32[2,8,256]{2,1,0:T(8,128)S(1)} %shard_map.37) | data formatting | bytes 32768
